TPU v7x, 256 devices: a whole 4x4x8 slice. The times are simulated.
256 devices in a mesh: seq: 32 (over y, z), tp: 8 (over x, core).
Axes of the slice: x: 4, y: 4, z: 8, core: 2. Of those that a mesh axis runs over, the one named last changes fastest.
Arguments:
- values_in: bfloat16 [16384, 8192], P('seq', 'tp'), may hold values from -6 to 6
- gates_in: bfloat16 [16384, 8192], P('seq', 'tp'), may hold values from -6 to 6
- keys_in: bfloat16 [16384, 1024], P('seq', 'tp'), may hold values from -6 to 6
- queries_in: bfloat16 [16384, 1024], P('seq', 'tp'), may hold values from -6 to 6
- log_decay: float32 [128, 16384], P('tp', 'seq'), may hold values from -2 to 0, as said below
- conv_values: float32 [4, 8192], P(None, 'tp'), may hold values from -3 to 3
- bias_values: float32 [8192], P('tp'), may hold values from -3 to 3
- conv_keys: float32 [4, 1024], P(None, 'tp'), may hold values from -3 to 3
- bias_keys: float32 [1024], P('tp'), may hold values from -3 to 3
- conv_queries: float32 [4, 1024], P(None, 'tp'), may hold values from -3 to 3
- bias_queries: float32 [1024], P('tp'), may hold values from -3 to 3
- skip_scale: float32 [128], P('tp'), may hold values from 0.5 to 1.5
- norm_gain: float32 [8192], P('tp'), may hold values from 0.1 to 1.9
- out_weight: bfloat16 [8192, 4096], P('tp'), may hold values from -0.09375 to 0.09375
Outputs:
- mixer_out: bfloat16 [16384, 4096], P('seq', 'tp')
Inputs may be any that keep to these rules, and one draw needn't show every extreme that they name: `log_decay`: every entry is below zero.
All inputs are finite; a program needn't handle non-finite values.
Results may differ from a plain program's by a relative error of at most 0.015.
Values may be sent and summed in bfloat16 or wider, within the bound.
A program may use at most 64 MiB of HBM per device.

v0:
```python
from functools import partial
import jax
import jax.numpy as jnp
from jax import lax
from jax.sharding import PartitionSpec as P

N = 128
HIGH = lax.Precision.HIGHEST
norm_epsilon = 1e-05


def passed_along(block, axis, distance):
    devices = range(lax.axis_size(axis))
    route = [(i - distance, i) for i in devices if i - distance in devices]
    return lax.ppermute(block, axis, route)


def causal_filter(padded, kernel_weights, conv_bias, row_total):
    width = kernel_weights.shape[0]
    running = jnp.broadcast_to(conv_bias[None, :], (row_total, conv_bias.shape[0]))
    for offset in range(width):
        running = running + kernel_weights[offset][None, :] * padded[
            offset : offset + row_total
        ].astype(jnp.float32)
    return jax.nn.silu(running).astype(jnp.bfloat16)


def block_terms(carried, inputs, per_group):
    values, keys_block, queries, logs = inputs
    row_total = values.shape[0]
    groups = keys_block.shape[1]
    cumulative = jnp.cumsum(logs, axis=1)
    scores = jnp.einsum("tgn,sgn->gts", queries, keys_block, preferred_element_type=jnp.float32)
    positions = lax.broadcasted_iota(jnp.int32, (row_total, row_total), 0)
    sources = lax.broadcasted_iota(jnp.int32, (row_total, row_total), 1)
    log_gaps = jnp.where(
        (positions >= sources)[None], cumulative[:, :, None] - cumulative[:, None, :], -jnp.inf
    )
    mixing = (
        jnp.exp(log_gaps).reshape(groups, per_group, row_total, row_total) * scores[:, None]
    ).astype(jnp.bfloat16)
    local_part = jnp.einsum("ghts,sghp->tghp", mixing, values, preferred_element_type=jnp.float32)
    growth = jnp.exp(cumulative).T.reshape(row_total, groups, per_group, 1)
    from_state = (
        jnp.einsum("tgn,ghnp->tghp", queries.astype(jnp.float32), carried, precision=HIGH) * growth
    )
    remaining = jnp.exp(cumulative[:, -1:] - cumulative).T.reshape(row_total, groups, per_group, 1)
    weighted_keys = keys_block.astype(jnp.float32)[:, :, None, :] * remaining
    fresh_state = jnp.einsum(
        "tghn,tghp->ghnp", weighted_keys, values.astype(jnp.float32), precision=HIGH
    )
    carried = jnp.exp(cumulative[:, -1]).reshape(groups, per_group, 1, 1) * carried + fresh_state
    return (carried, local_part + from_state)


def shards(
    values_in,
    gates_in,
    keys_in,
    queries_in,
    log_decay,
    conv_values,
    bias_values,
    conv_keys,
    bias_keys,
    conv_queries,
    bias_queries,
    skip_scale,
    norm_gain,
    out_weight,
):
    row_total = values_in.shape[0]
    head_count = log_decay.shape[0]
    inner_width = values_in.shape[1]
    head_size = inner_width // head_count
    key_width = keys_in.shape[1]
    groups = key_width // N
    per_group = head_count // groups
    margin = conv_values.shape[0] - 1
    rim_send = jnp.concatenate(
        [
            values_in[row_total - margin :],
            keys_in[row_total - margin :],
            queries_in[row_total - margin :],
        ],
        axis=1,
    )
    rim_rows = passed_along(rim_send, "seq", 1)
    values = causal_filter(
        jnp.concatenate([rim_rows[:, :inner_width], values_in], axis=0),
        conv_values,
        bias_values,
        row_total,
    )
    keys_all = causal_filter(
        jnp.concatenate([rim_rows[:, inner_width : inner_width + key_width], keys_in], axis=0),
        conv_keys,
        bias_keys,
        row_total,
    )
    queries_all = causal_filter(
        jnp.concatenate([rim_rows[:, inner_width + key_width :], queries_in], axis=0),
        conv_queries,
        bias_queries,
        row_total,
    )
    block_rows = min(row_total, 512)
    block_count = row_total // block_rows
    value_blocks = values.reshape(block_count, block_rows, groups, per_group, head_size)
    key_blocks = keys_all.reshape(block_count, block_rows, groups, N)
    query_blocks = queries_all.reshape(block_count, block_rows, groups, N)
    log_blocks = log_decay.reshape(head_count, block_count, block_rows).transpose(1, 0, 2)
    initial = jnp.zeros((groups, per_group, N, head_size), jnp.float32)
    local_end, outputs = lax.scan(
        partial(block_terms, per_group=per_group),
        initial,
        (value_blocks, key_blocks, query_blocks, log_blocks),
    )
    cumulative = jnp.cumsum(log_decay, axis=1)
    device_log = cumulative[:, -1]
    flat_end = local_end.reshape(head_count, N * head_size)
    all_logs = lax.all_gather(device_log[None, :], "seq", axis=0, tiled=True)
    inclusive = jnp.cumsum(all_logs, axis=0)
    own_index = lax.axis_index("seq")
    before_mine = lax.dynamic_index_in_dim(inclusive - all_logs, own_index, 0, keepdims=False)
    pieces = lax.all_gather(flat_end[None].astype(jnp.bfloat16), "seq", axis=0, tiled=True).astype(
        jnp.float32
    )
    shard_ids = jnp.arange(pieces.shape[0], dtype=jnp.int32)
    through_shard = jnp.take(inclusive, shard_ids, axis=0)
    exponent = jnp.where(
        (shard_ids < own_index)[:, None], before_mine[None, :] - through_shard, -jnp.inf
    )
    incoming = jnp.zeros_like(flat_end) + jnp.einsum(
        "kh,khm->hm", jnp.exp(exponent), pieces, precision=HIGH
    )
    incoming = incoming.reshape(groups, per_group, N, head_size)
    growth = jnp.exp(cumulative).T.reshape(row_total, groups, per_group, 1)
    query_rows = queries_all.reshape(row_total, groups, N).astype(jnp.float32)
    from_before = jnp.einsum("tgn,ghnp->tghp", query_rows, incoming, precision=HIGH) * growth
    mixed = outputs.reshape(row_total, groups, per_group, head_size) + from_before
    mixed = mixed + skip_scale.reshape(groups, per_group)[None, :, :, None] * values.reshape(
        row_total, groups, per_group, head_size
    ).astype(jnp.float32)
    gated_rows = mixed.reshape(row_total, groups, per_group * head_size) * jax.nn.silu(
        gates_in.reshape(row_total, groups, per_group * head_size).astype(jnp.float32)
    )
    mean_square = jnp.mean(gated_rows * gated_rows, axis=-1, keepdims=True)
    normed = (
        (
            gated_rows
            * lax.rsqrt(mean_square + norm_epsilon)
            * norm_gain.reshape(groups, per_group * head_size)
        )
        .astype(jnp.bfloat16)
        .reshape(row_total, inner_width)
    )
    local_sum = jnp.dot(normed, out_weight, preferred_element_type=jnp.float32)
    summed = lax.psum(local_sum.astype(jnp.bfloat16), "tp").astype(jnp.float32)
    column_width = summed.shape[1] // lax.axis_size("tp")
    result = lax.dynamic_slice_in_dim(summed, lax.axis_index("tp") * column_width, column_width, 1)
    return result.astype(jnp.bfloat16)


def solution(mesh):
    placed = (
        P("seq", "tp"),
        P("seq", "tp"),
        P("seq", "tp"),
        P("seq", "tp"),
        P("tp", "seq"),
        P(None, "tp"),
        P("tp"),
        P(None, "tp"),
        P("tp"),
        P(None, "tp"),
        P("tp"),
        P("tp"),
        P("tp"),
        P("tp", None),
    )
    return jax.shard_map(
        shards, mesh=mesh, in_specs=placed, out_specs=P("seq", "tp"), check_vma=False
    )
```

profile of v0, /device:TPU:8, one launch (start us, length us, event | category | flops | bytes accessed | tf_op | source)
XLA Modules:
  0.0 248.3 jit_solution(196115072066289706)
XLA Ops:
  6.5 0.0 all-gather.3.cloned.1.call-start
  6.6 0.8 slice.96
  7.4 0.7 slice.97
  8.1 0.7 slice.98
  8.8 0.3 copy.48
  9.0 3.8 %collective-permute-start = (bf16[3,1280]{0,1:T(8,128)(2,1)S(1)}, bf16[3,1280]{0,1:T(8,128)(2,1)S(1)}, u32[]{:S(2)}, u32[]{:S(2)}) collective-permute-start(bf16[3,1280]{0,1:T(8,128)(2,1)S(1)} %copy.48), channel_id=1, source_target_pairs={{0,8},{8,16},{16,24},{24,32},{32,40},{40,48},{48,56},{56,64},{64,7... | collective-permute-start | bytes 23048 | tf_op jit(solution)/shard_map/ppermute | solution.py:15
  12.9 1.2 reduce-window.12
  14.0 0.2 slice_reduce_fusion
  14.2 0.1 copy_bitcast_fusion.1
  14.3 0.2 slice_reduce_fusion.1
  14.5 0.9 fusion.41
  15.4 0.8 slice_bitcast_fusion.3
  16.2 0.1 exponential_bitcast_fusion.1
  16.3 1.5 copy.49
  17.8 6.5 %collective-permute-done = bf16[3,1280]{0,1:T(8,128)(2,1)S(1)} collective-permute-done((bf16[3,1280]{0,1:T(8,128)(2,1)S(1)}, bf16[3,1280]{0,1:T(8,128)(2,1)S(1)}, u32[]{:S(2)}, u32[]{:S(2)}) %collective-permute-start) | collective-permute-done | bytes 7712 | tf_op jit(solution)/shard_map/ppermute | solution.py:15
  24.4 0.1 copy.54
  24.5 0.2 fusion.39
  24.7 2.7 %multiply_convert_fusion.3 = bf16[512,1024]{0,1:T(8,128)(2,1)S(1)} fusion(bf16[512,1024]{0,1:T(8,128)(2,1)S(1)} %copy.49, bf16[3,1024]{0,1:T(8,128)(2,1)S(1)} %slice.127, f32[1024]{0:T(1024)S(1)} %bitcast.91, f32[1024]{0:T(1024)S(1)} %bitcast.92, f32[1024]{0:T(1024)S(1)} %bitcast.90, f32[1024]{0:T(1024)S(1)} %bitcast.89, f32[1024]{0:T(1024)S(1)} %copy-done.7), kind=kLoop, calls=%fused_computation.25 | loop fusion | flops 13631488 | bytes 2123776 | tf_op jit(solution)/shard_map/convert_element_type | solution.py:25
  27.4 2.4 fusion.18
  29.9 0.3 copy.55
  30.1 1.2 convert_element_type.126
  31.4 0.0 all-reduce.3.cloned.1.call-start
  31.4 0.6 dynamic-slice.1
  32.7 0.2 dynamic-update-slice
  32.9 62.4 %all-reduce = f32[512]{0:T(512)S(1)} all-reduce(f32[512]{0:T(512)S(1)} %dynamic-update-slice), channel_id=2, replica_groups=mesh['seq'=32,'tp'=8] {'seq'}, use_global_device_ids=true, to_apply=%add | all-reduce | flops 512 | bytes 4096
  95.4 0.1 reshape.221
  95.4 0.1 reduce_window_sum.40
  95.5 0.6 gather_fusion
  96.1 0.1 exponential_bitcast_fusion.2
  96.2 0.1 copy.58
  96.3 1.3 copy.57
  97.6 0.8 iota_compare_fusion
  98.4 0.1 copy.53
  98.5 0.2 multiply_convert_fusion.6
  98.7 0.3 fusion.42
  99.0 1.0 fusion.25
  100.0 5.8 %fusion.2 = f32[16,64,512]{2,1,0:T(8,128)} fusion(bf16[512,16,64]{0,2,1:T(8,128)(2,1)S(1)} %bitcast.86, f32[512,512]{1,0:T(8,128)S(1)} %fusion.42, f32[16,512]{1,0:T(8,128)S(1)} %copy_bitcast_fusion.1, pred[512,512]{1,0:T(8,128)(4,1)S(1)} %copy-done.4), kind=kOutput, calls=%fused_computation.4 | convolution fusion | flops 553648128 | bytes 4489216 | tf_op jit(solution)/shard_map/while/body/eval_jaxpr/ghts,sghp->tghp/dot_general | solution.py:42
  105.8 22.5 %all-gather.3.cloned.1.call-done = bf16[32,16,8192]{2,1,0:T(8,128)(2,1)} async-done(((bf16[1,16,8192]{2,1,0:T(8,128)(2,1)}), bf16[32,16,8192]{2,1,0:T(8,128)(2,1)}) %all-gather.3.cloned.1.call-update) | async-done | bytes 8388624 | tf_op jit(solution)/shard_map/all_gather | solution.py:126
  128.3 16.9 %fusion = f32[16,1,8192]{2,1,0:T(1,128)S(1)} fusion(f32[32,16,1]{0,2,1:T(1,128)S(1)} %copy.58, bf16[32,16,8192]{2,1,0:T(8,128)(2,1)} %all-gather.3.cloned.1.call-done), kind=kOutput, calls=%fused_computation.2 | convolution fusion | flops 50331648 | bytes 8914944 | tf_op jit(solution)/shard_map/kh,khm->hm/dot_general | solution.py:134
  145.2 1.1 copy.73
  146.3 2.5 reshape.210
  148.7 3.2 %fusion.31 = f32[16,64,512]{2,1,0:T(8,128)S(1)} fusion(f32[16,128,64]{2,1,0:T(8,128)} %reshape.210, bf16[512,128]{1,0:T(8,128)(2,1)S(1)} %multiply_convert_fusion.6), kind=kOutput, calls=%fused_computation.54 | convolution fusion | flops 805306368 | bytes 2752512 | tf_op jit(solution)/shard_map/tgn,ghnp->tghp/dot_general | solution.py:140
  152.0 1.0 fusion.10
  153.0 0.2 copy-done.1
  153.2 0.7 multiply_reduce_fusion
  153.9 9.7 %convolution_convert_fusion = bf16[512,4096]{1,0:T(8,128)(2,1)} fusion(bf16[1024,4096]{1,0:T(8,128)(2,1)} %param.27, f32[512,1024]{0,1:T(8,128)S(1)} %get-tuple-element.18, f32[1024]{0:T(1024)S(1)} %copy-done.12, f32[512]{0:T(512)S(1)} %add_rsqrt_fusion), kind=kOutput, calls=%fused_computation.6 | convolution fusion | flops 4298637312 | bytes 14686208 | tf_op jit(solution)/shard_map/dot_general | solution.py:158
  163.7 75.9 %all-reduce.3.cloned.1.call-done = bf16[512,4096]{1,0:T(8,128)(2,1)} async-done(((bf16[512,4096]{1,0:T(8,128)(2,1)}), bf16[512,4096]{1,0:T(8,128)(2,1)}) %all-reduce.3.cloned.1.call-update) | async-done | bytes 4194320 | tf_op jit(solution)/shard_map/psum | solution.py:159
  239.6 1.9 convert_convert_fusion
  (43 shorter events, 0.2 us)
Async XLA Ops:
  6.5 6.3 %copy-start = (f32[16,512]{1,0:T(8,128)S(1)}, f32[16,512]{1,0:T(8,128)}, u32[]{:S(2)}) copy-start(f32[16,512]{1,0:T(8,128)} %param.18) | copy-start | bytes 98308
  6.5 17.9 %copy-start.5 = (bf16[512,128]{1,0:T(8,128)(2,1)S(1)}, bf16[512,128]{1,0:T(8,128)(2,1)}, u32[]{:S(2)}) copy-start(bf16[512,128]{1,0:T(8,128)(2,1)} %param.16) | copy-start | bytes 393220
  6.5 17.9 %copy-start.9 = (f32[128]{0:T(128)S(1)}, f32[128]{0:T(128)}, u32[]{:S(2)}) copy-start(f32[128]{0:T(128)} %param.22) | copy-start | bytes 1540
  6.5 18.2 %copy-start.7 = (f32[1024]{0:T(1024)S(1)}, f32[1024]{0:T(1024)}, u32[]{:S(2)}) copy-start(f32[1024]{0:T(1024)} %param.20) | copy-start | bytes 12292
  6.5 121.8 %all-gather.3.cloned.1.call-start = ((), (), s32[]{:S(2)}) async-start(), calls=%async_computation | async-start | bytes 8650752 | tf_op jit(solution)/shard_map/all_gather | solution.py:126
  9.0 15.4 %collective-permute-start = (bf16[3,1280]{0,1:T(8,128)(2,1)S(1)}, bf16[3,1280]{0,1:T(8,128)(2,1)S(1)}, u32[]{:S(2)}, u32[]{:S(2)}) collective-permute-start(bf16[3,1280]{0,1:T(8,128)(2,1)S(1)} %copy.48), channel_id=1, source_target_pairs={{0,8},{8,16},{16,24},{24,32},{32,40},{40,48},{48,56},{56,64},{64,7... | collective-permute-start | bytes 23048 | tf_op jit(solution)/shard_map/ppermute | solution.py:15
  27.4 4.0 %copy-start.13 = (u32[256]{0:T(256)S(1)}, u32[256]{0:T(256)}, u32[]{:S(2)}) copy-start(u32[256]{0:T(256)} %constant.80) | copy-start | bytes 3076
  27.4 68.9 %copy-start.3 = (bf16[512,1024]{1,0:T(8,128)(2,1)S(1)}, bf16[512,1024]{1,0:T(8,128)(2,1)}, u32[]{:S(2)}) copy-start(bf16[512,1024]{1,0:T(8,128)(2,1)} %param.15) | copy-start | bytes 3145732
  29.8 68.6 %copy-start.8 = (f32[4,128]{1,0:T(4,128)S(1)}, f32[4,128]{1,0:T(4,128)}, u32[]{:S(2)}) copy-start(f32[4,128]{1,0:T(4,128)} %param.23) | copy-start | bytes 6148
  29.8 68.7 %copy-start.6 = (bf16[512,128]{1,0:T(8,128)(2,1)S(1)}, bf16[512,128]{1,0:T(8,128)(2,1)}, u32[]{:S(2)}) copy-start(bf16[512,128]{1,0:T(8,128)(2,1)} %param.17) | copy-start | bytes 393220
  29.8 68.7 %copy-start.10 = (f32[128]{0:T(128)S(1)}, f32[128]{0:T(128)}, u32[]{:S(2)}) copy-start(f32[128]{0:T(128)} %param.24) | copy-start | bytes 1540
  31.4 208.2 %all-reduce.3.cloned.1.call-start = ((), (), s32[]{:S(2)}) async-start(), calls=%async_computation.1 | async-start | bytes 8388608 | tf_op jit(solution)/shard_map/psum | solution.py:159
  98.5 1.5 copy-start.4
  146.3 5.7 %copy-start.11 = (f32[16]{0:T(128)S(1)}, f32[16]{0:T(128)}, u32[]{:S(2)}) copy-start(f32[16]{0:T(128)} %param.25) | copy-start | bytes 196
  148.7 3.2 %copy-start.2 = (f32[16,64,512]{2,1,0:T(8,128)S(1)}, f32[16,64,512]{2,1,0:T(8,128)}, u32[]{:S(2)}) copy-start(f32[16,64,512]{2,1,0:T(8,128)} %fusion.2) | copy-start | bytes 6291460
  152.0 1.2 copy-start.1
  153.2 0.7 copy-start.12
Sparse Core Ops, SparseCore 0:
  31.5 96.7 all-gather.2
  163.8 75.7 all-reduce.2
where the time goes:
time: 249 us; the launch traced here: 248 us
  waiting for transfers between devices  105 us (42%)
  blocking collectives  62.4 us (25%)
  matrix products  39.3 us (16%)
  local copies, waits for them, and re-layouts  14.4 us (6%)
  between operations  14.3 us (6%)
  other arithmetic  8.96 us (4%)
  starting transfers between devices  3.9 us (2%)
    psum x1, waiting for transfers between devices, shards(): summed = lax.psum(local_sum.astype(jnp.bfloat16), 'tp').astype(jnp.float32)  75.9 us
    unnamed x1, blocking collectives  62.4 us
    all_gather x1, waiting for transfers between devices, shards(): lax.all_gather(flat_end[None].astype(jnp.bfloat16), 'seq', axis=0, tiled=...  22.5 us
    dot_general x1, matrix products, shards(): jnp.einsum('kh,khm->hm', jnp.exp(exponent), pieces, precision=HIGH)  16.9 us
    dot_general x1, matrix products, shards(): local_sum = jnp.dot(normed, out_weight, preferred_element_type=jnp.float32)  9.74 us
    ppermute x1, waiting for transfers between devices, passed_along(): return lax.ppermute(block, axis, route)  6.53 us
    dot_general x1, matrix products, block_terms(): jnp.einsum('ghts,sghp->tghp', mixing, values, preferred_element_type=jnp....  5.8 us
  transfers between devices with their start and end apart: 3, of which 3 were waited for; matrix products, arithmetic and copies ran while one was open for 7% of the time, Pallas kernels for 0%

commit v1 on v0

--- a/solution.py
+++ b/solution.py
@@ -123,9 +123,20 @@
     inclusive = jnp.cumsum(all_logs, axis=0)
     own_index = lax.axis_index("seq")
     before_mine = lax.dynamic_index_in_dim(inclusive - all_logs, own_index, 0, keepdims=False)
-    pieces = lax.all_gather(flat_end[None].astype(jnp.bfloat16), "seq", axis=0, tiled=True).astype(
-        jnp.float32
-    )
+
+    def counts_work(work_x):
+        tall = jnp.concatenate(
+            lax.all_to_all(
+                jnp.stack(tuple((work_x for _ in range(lax.axis_size("seq")))), 0),
+                "seq",
+                split_axis=0,
+                concat_axis=0,
+            ),
+            0,
+        )
+        return tall
+
+    pieces = counts_work(flat_end[None].astype(jnp.bfloat16)).astype(jnp.float32)
     shard_ids = jnp.arange(pieces.shape[0], dtype=jnp.int32)
     through_shard = jnp.take(inclusive, shard_ids, axis=0)
     exponent = jnp.where(

time: 249 us -> 420 us (1.69)
  blocking collectives: 62.4 us -> 239 us
  waiting for transfers between devices: 105 us -> 87.4 us
  starting transfers between devices: 3.9 us -> 13 us
    unnamed x1, blocking collectives: 62.4 us -> 239 us
    all_gather x1 -> x0, waiting for transfers between devices: 22.5 us -> none  [shards(): lax.all_gather(flat_end[None].astype(jnp.bfloat16), 'seq', axis=0, tiled=...]
    all_to_all x0 -> x1, starting transfers between devices: none -> 9.09 us  [counts_work(): lax.all_to_all(jnp.stack(tuple((work_x for _ in range(lax.axis_size('seq'...]
    psum x1, waiting for transfers between devices: 75.9 us -> 80.9 us  [shards(): summed = lax.psum(local_sum.astype(jnp.bfloat16), 'tp').astype(jnp.float32)]
    another operation x4 -> x5, local copies, waits for them, and re-layouts: 2.61 us -> 6.84 us  [the longest x1 4.24 us: counts_work(): jnp.stack(tuple((work_x for _ in range(lax.axis_size('seq')))), 0)]
  transfers between devices with their start and end apart: 3 -> 3, of which waited for: 3 -> 2; matrix products, arithmetic and copies ran while one was open for 7% -> 4% of each run, Pallas kernels for 0% -> 0%
where the time goes in v1:
time: 420 us; the launch traced here: 419 us
  blocking collectives  239 us (57%)
  waiting for transfers between devices  87.4 us (21%)
  matrix products  39.3 us (9%)
  local copies, waits for them, and re-layouts  17.9 us (4%)
  between operations  14.4 us (3%)
  starting transfers between devices  13 us (3%)
  other arithmetic  8.93 us (2%)
    unnamed x1, blocking collectives  239 us
    psum x1, waiting for transfers between devices, shards(): summed = lax.psum(local_sum.astype(jnp.bfloat16), 'tp').astype(jnp.float32)  80.9 us
    dot_general x1, matrix products, shards(): jnp.einsum('kh,khm->hm', jnp.exp(exponent), pieces, precision=HIGH)  16.9 us
    dot_general x1, matrix products, shards(): local_sum = jnp.dot(normed, out_weight, preferred_element_type=jnp.float32)  9.73 us
    all_to_all x1, starting transfers between devices, counts_work(): lax.all_to_all(jnp.stack(tuple((work_x for _ in range(lax.axis_size('seq'...  9.09 us
  transfers between devices with their start and end apart: 3, of which 2 were waited for; matrix products, arithmetic and copies ran while one was open for 4% of the time, Pallas kernels for 0%

profile of v1, /device:TPU:8, one launch (start us, length us, event | category | flops | bytes accessed | tf_op | source)
XLA Modules:
  0.0 419.5 jit_solution(9266381358810345973)
XLA Ops:
  6.5 0.8 slice.96
  7.3 0.7 slice.97
  8.0 0.7 slice.98
  8.7 0.3 copy.48
  8.9 3.8 collective-permute-start
  12.8 1.2 reduce-window.12
  14.0 0.2 slice_reduce_fusion
  14.2 0.1 copy_bitcast_fusion.1
  14.2 0.2 slice_reduce_fusion.1
  14.4 0.9 fusion.41
  15.3 0.8 slice_bitcast_fusion.3
  16.2 0.1 exponential_bitcast_fusion.1
  16.3 1.5 copy.49
  17.8 6.5 %collective-permute-done = bf16[3,1280]{0,1:T(8,128)(2,1)S(1)} collective-permute-done((bf16[3,1280]{0,1:T(8,128)(2,1)S(1)}, bf16[3,1280]{0,1:T(8,128)(2,1)S(1)}, u32[]{:S(2)}, u32[]{:S(2)}) %collective-permute-start) | collective-permute-done | bytes 7712 | tf_op jit(solution)/shard_map/ppermute | solution.py:15
  24.3 0.1 copy.54
  24.4 0.2 fusion.39
  24.6 2.7 multiply_convert_fusion.3
  27.3 2.4 fusion.18
  29.7 0.3 copy.55
  30.0 0.5 convert_element_type.125
  30.5 4.2 %stack.2 = bf16[32,1,16,8192]{3,2,1,0:T(8,128)(2,1)} broadcast(bf16[16,8192]{1,0:T(8,128)(2,1)S(1)} %convert_element_type.125), dimensions={2,3} | broadcast | bytes 8650752 | tf_op jit(solution)/shard_map/stack | solution.py:130
  34.7 9.1 %all-to-all-start = ((bf16[32,1,16,8192]{3,2,1,0:T(8,128)(2,1)}), bf16[32,1,16,8192]{3,2,1,0:T(8,128)(2,1)}, u32[]{:S(2)}, u32[]{:S(2)}) async-start(bf16[32,1,16,8192]{3,2,1,0:T(8,128)(2,1)} %stack.2), calls=%async_computation | async-start | bytes 16777216 | tf_op jit(solution)/shard_map/all_to_all | solution.py:129
  43.9 0.0 all-reduce.3.cloned.1.call-start
  43.9 0.6 dynamic-slice.1
  45.2 0.2 dynamic-update-slice
  45.4 238.6 %all-reduce = f32[512]{0:T(512)S(1)} all-reduce(f32[512]{0:T(512)S(1)} %dynamic-update-slice), channel_id=2, replica_groups=mesh['seq'=32,'tp'=8] {'seq'}, use_global_device_ids=true, to_apply=%add | all-reduce | flops 512 | bytes 4096
  284.0 0.1 reshape.224
  284.1 0.1 reduce_window_sum.40
  284.2 0.6 gather_fusion
  284.8 0.1 exponential_bitcast_fusion.2
  284.9 0.1 copy.58
  285.0 1.3 copy.57
  286.3 0.8 iota_compare_fusion
  287.1 0.1 copy.53
  287.2 0.2 multiply_convert_fusion.6
  287.4 0.3 fusion.42
  287.7 1.0 fusion.25
  288.7 5.8 %fusion.2 = f32[16,64,512]{2,1,0:T(8,128)} fusion(bf16[512,16,64]{0,2,1:T(8,128)(2,1)S(1)} %bitcast.87, f32[512,512]{1,0:T(8,128)S(1)} %fusion.42, f32[16,512]{1,0:T(8,128)S(1)} %copy_bitcast_fusion.1, pred[512,512]{1,0:T(8,128)(4,1)S(1)} %copy-done.4), kind=kOutput, calls=%fused_computation.4 | convolution fusion | flops 553648128 | bytes 4489216 | tf_op jit(solution)/shard_map/while/body/eval_jaxpr/ghts,sghp->tghp/dot_general | solution.py:42
  294.5 16.9 %fusion = f32[16,1,8192]{2,1,0:T(1,128)S(1)} fusion(f32[32,16,1]{0,2,1:T(1,128)S(1)} %copy.58, bf16[32,16,8192]{2,1,0:T(8,128)(2,1)} %bitcast.23), kind=kOutput, calls=%fused_computation.2 | convolution fusion | flops 50331648 | bytes 8914944 | tf_op jit(solution)/shard_map/kh,khm->hm/dot_general | solution.py:145
  311.4 1.1 copy.73
  312.5 2.4 reshape.213
  314.9 3.2 fusion.31
  318.2 1.0 fusion.10
  319.2 0.2 copy-done.1
  319.4 0.7 multiply_reduce_fusion
  320.1 9.7 %convolution_convert_fusion = bf16[512,4096]{1,0:T(8,128)(2,1)} fusion(bf16[1024,4096]{1,0:T(8,128)(2,1)} %param.27, f32[512,1024]{0,1:T(8,128)S(1)} %get-tuple-element.18, f32[1024]{0:T(1024)S(1)} %copy-done.12, f32[512]{0:T(512)S(1)} %add_rsqrt_fusion), kind=kOutput, calls=%fused_computation.6 | convolution fusion | flops 4298637312 | bytes 14686208 | tf_op jit(solution)/shard_map/dot_general | solution.py:169
  329.9 80.9 %all-reduce.3.cloned.1.call-done = bf16[512,4096]{1,0:T(8,128)(2,1)} async-done(((bf16[512,4096]{1,0:T(8,128)(2,1)}), bf16[512,4096]{1,0:T(8,128)(2,1)}) %all-reduce.3.cloned.1.call-update) | async-done | bytes 4194320 | tf_op jit(solution)/shard_map/psum | solution.py:170
  410.7 1.9 convert_convert_fusion
  (43 shorter events, 0.2 us)
Async XLA Ops:
  6.5 6.3 %copy-start = (f32[16,512]{1,0:T(8,128)S(1)}, f32[16,512]{1,0:T(8,128)}, u32[]{:S(2)}) copy-start(f32[16,512]{1,0:T(8,128)} %param.18) | copy-start | bytes 98308
  6.5 17.8 %copy-start.5 = (bf16[512,128]{1,0:T(8,128)(2,1)S(1)}, bf16[512,128]{1,0:T(8,128)(2,1)}, u32[]{:S(2)}) copy-start(bf16[512,128]{1,0:T(8,128)(2,1)} %param.16) | copy-start | bytes 393220
  6.5 17.9 %copy-start.9 = (f32[128]{0:T(128)S(1)}, f32[128]{0:T(128)}, u32[]{:S(2)}) copy-start(f32[128]{0:T(128)} %param.22) | copy-start | bytes 1540
  6.5 18.1 %copy-start.7 = (f32[1024]{0:T(1024)S(1)}, f32[1024]{0:T(1024)}, u32[]{:S(2)}) copy-start(f32[1024]{0:T(1024)} %param.20) | copy-start | bytes 12292
  8.9 15.4 %collective-permute-start = (bf16[3,1280]{0,1:T(8,128)(2,1)S(1)}, bf16[3,1280]{0,1:T(8,128)(2,1)S(1)}, u32[]{:S(2)}, u32[]{:S(2)}) collective-permute-start(bf16[3,1280]{0,1:T(8,128)(2,1)S(1)} %copy.48), channel_id=1, source_target_pairs={{0,8},{8,16},{16,24},{24,32},{32,40},{40,48},{48,56},{56,64},{64,7... | collective-permute-start | bytes 23048 | tf_op jit(solution)/shard_map/ppermute | solution.py:15
  34.7 9.2 %copy-start.13 = (u32[256]{0:T(256)S(1)}, u32[256]{0:T(256)}, u32[]{:S(2)}) copy-start(u32[256]{0:T(256)} %constant.80) | copy-start | bytes 3076
  34.7 250.2 %copy-start.3 = (bf16[512,1024]{1,0:T(8,128)(2,1)S(1)}, bf16[512,1024]{1,0:T(8,128)(2,1)}, u32[]{:S(2)}) copy-start(bf16[512,1024]{1,0:T(8,128)(2,1)} %param.15) | copy-start | bytes 3145732
  34.7 259.8 %all-to-all-start = ((bf16[32,1,16,8192]{3,2,1,0:T(8,128)(2,1)}), bf16[32,1,16,8192]{3,2,1,0:T(8,128)(2,1)}, u32[]{:S(2)}, u32[]{:S(2)}) async-start(bf16[32,1,16,8192]{3,2,1,0:T(8,128)(2,1)} %stack.2), calls=%async_computation | async-start | bytes 16777216 | tf_op jit(solution)/shard_map/all_to_all | solution.py:129
  43.8 243.3 %copy-start.8 = (f32[4,128]{1,0:T(4,128)S(1)}, f32[4,128]{1,0:T(4,128)}, u32[]{:S(2)}) copy-start(f32[4,128]{1,0:T(4,128)} %param.23) | copy-start | bytes 6148
  43.8 243.3 %copy-start.6 = (bf16[512,128]{1,0:T(8,128)(2,1)S(1)}, bf16[512,128]{1,0:T(8,128)(2,1)}, u32[]{:S(2)}) copy-start(bf16[512,128]{1,0:T(8,128)(2,1)} %param.17) | copy-start | bytes 393220
  43.8 243.3 %copy-start.10 = (f32[128]{0:T(128)S(1)}, f32[128]{0:T(128)}, u32[]{:S(2)}) copy-start(f32[128]{0:T(128)} %param.24) | copy-start | bytes 1540
  43.9 366.9 %all-reduce.3.cloned.1.call-start = ((), (), s32[]{:S(2)}) async-start(), calls=%async_computation.1 | async-start | bytes 8388608 | tf_op jit(solution)/shard_map/psum | solution.py:170
  287.2 1.5 copy-start.4
  312.5 5.7 %copy-start.11 = (f32[16]{0:T(128)S(1)}, f32[16]{0:T(128)}, u32[]{:S(2)}) copy-start(f32[16]{0:T(128)} %param.25) | copy-start | bytes 196
  314.9 3.2 copy-start.2
  318.2 1.2 copy-start.1
  319.4 0.7 copy-start.12
Sparse Core Ops, SparseCore 0:
  330.0 80.7 all-reduce.2
